TPU v7x, 32 devices: a whole 2x2x4 slice. The times are simulated.
32 devices in a mesh: region: 8 (over z, core), member: 4 (over y, x).
Axes of the slice: x: 2, y: 2, z: 4, core: 2. Of those that a mesh axis runs over, the one named last changes fastest.
Arguments:
- positions: float32 [3, 12288], P(None, ('region', 'member'))
- forces: float32 [3, 12288], P(None, ('region', 'member')), may hold values from -6 to 6
- blob_platelet: int32 [12288], P(('region', 'member')), may hold values from 0 to 8, as said below
- blob_rank: int32 [12288], P(('region', 'member')), may hold values from 0 to 161, as said below
- platelet_owner: int32 [64], P('region'), may hold values from 0 to 7, as said below
- pair_list: int32 [96, 8], P(('region', 'member')), may hold values from 0 to 23, as said below
- pair_count: int32 [96], P(('region', 'member')), may hold values from 1 to 8, as said below
- preconditioner: bfloat16 [64, 486, 486], P(('region', 'member')), may hold values from -0.25 to 0.25
Outputs:
- blob_velocity: float32 [3, 12288], P(None, ('region', 'member'))
- body_velocity: float32 [64, 486], P(('region', 'member'))
Inputs may be any that keep to these rules, and one draw needn't show every extreme that they name: `blob_platelet`: in each slab every platelet id below 8 appears on exactly 162 slots, and 8 marks an empty slot. Every device holds exactly 324 live blobs, of which at most 121 belong to platelets whose owner slots lie on one member; that bound is met in every slab. `blob_rank`: the 162 blobs of one platelet have distinct ranks; empty slots have rank 0. `platelet_owner`: the 8 entries of one slab are a permutation; owner slot o lies on member o // 2 of that slab. `pair_list`: the entries of one target tile are distinct, and entry 0 is the tile itself, 6 plus its index within its slab. `pair_count`: some tile has 8 in every draw.
All inputs are finite; a program needn't handle non-finite values.
Results may differ from a plain program's by a relative error of at most 0.0029.
Values sent between devices are 32-bit elements; how exact they have to be, the bound alone decides.
A program may use at most 64 MiB of HBM per device.

v0:
```python
import math
import jax
import jax.numpy as jnp
from jax import lax
from jax.sharding import PartitionSpec as P

TILE = 128
PB = 162
PLAT_DEV = 2
soft_square = 1.0


def padded(cells, sides, width):
    for axis, dim in sides:
        count = lax.axis_size(axis)
        ends = count - 1
        head = lax.slice_in_dim(cells, 0, width, axis=dim)
        tail = lax.slice_in_dim(cells, cells.shape[dim] - width, cells.shape[dim], axis=dim)
        cells = jnp.concatenate(
            [
                lax.ppermute(tail, axis, [(i, (i + 1) % count) for i in range(ends)]),
                cells,
                lax.ppermute(head, axis, [((i + 1) % count, i) for i in range(ends)]),
            ],
            axis=dim,
        )
    return cells


def stokes_sum(targets, sources, pushes):
    force = pushes[:, :, None, :]
    separation = targets[:, :, :, None] - sources[:, :, None, :]
    dist_square = jnp.sum(separation * separation, axis=0)
    force_along = jnp.sum(separation * force, axis=0)
    kernel_weight = 1.0 / (
        8.0 * math.pi * (dist_square + soft_square) * jnp.sqrt(dist_square + soft_square)
    )
    direct = ((dist_square + 2.0 * soft_square) * force + separation * force_along) * kernel_weight
    flip_source = jnp.array([1.0, 1.0, -1.0], jnp.float32)[:, None, None]
    flip_pair = jnp.array([1.0, 1.0, -1.0], jnp.float32)[:, None, None, None]
    unit_normal = jnp.array([0.0, 0.0, 1.0], jnp.float32)[:, None, None, None]
    height = sources[2][:, None, :]
    image_gap = targets[:, :, :, None] - (sources * flip_source)[:, :, None, :]
    image_square = jnp.sum(image_gap * image_gap, axis=0)
    inverse_one = 1.0 / jnp.sqrt(image_square)
    inverse_three = inverse_one * inverse_one * inverse_one
    inverse_five = inverse_three * inverse_one * inverse_one
    image_along = jnp.sum(image_gap * force, axis=0)
    mirrored = force * flip_pair
    mirror_along = jnp.sum(image_gap * mirrored, axis=0)
    normal_gap = image_gap[2]
    stokes_image = force * inverse_one + image_gap * image_along * inverse_three
    doublet = height * (mirrored * inverse_three - 3.0 * image_gap * mirror_along * inverse_five)
    doublet = doublet + unit_normal * mirror_along * inverse_three
    doublet = doublet - (mirrored * normal_gap + image_gap * mirrored[2]) * inverse_three
    doublet = doublet + 3.0 * image_gap * normal_gap * mirror_along * inverse_five
    wall_term = (2.0 * height * doublet - stokes_image) * (1.0 / (8.0 * math.pi))
    return jnp.sum(direct + wall_term, axis=3)


def on_device(
    positions,
    forces,
    blob_platelet,
    blob_rank,
    platelet_owner,
    pair_list,
    pair_count,
    preconditioner,
):
    blob_count = positions.shape[1]
    plate_count = platelet_owner.shape[0]
    is_live = blob_platelet < plate_count
    live_mask = is_live.astype(jnp.float32)
    own_blobs = jnp.concatenate([positions, forces * live_mask[None, :]], 0)
    region_all = lax.all_gather(own_blobs, "member", axis=1, tiled=True)
    extended = padded(region_all, (("region", 1),), region_all.shape[1] // 2)
    ext_blocks = extended.reshape(6, extended.shape[1] // TILE, TILE)
    targets = positions.reshape(3, blob_count // TILE, TILE)
    pair_rounds = jnp.max(pair_count)

    def one_slot(pair_slot, accumulated):
        source_ids = lax.dynamic_index_in_dim(pair_list, pair_slot, 1, keepdims=False)
        picked = jnp.take(ext_blocks, source_ids, axis=1)
        keep_mask = (pair_slot < pair_count).astype(jnp.float32)
        return accumulated + keep_mask[None, :, None] * stokes_sum(targets, picked[:3], picked[3:])

    velocity = lax.fori_loop(0, pair_rounds, one_slot, jnp.zeros(targets.shape, jnp.float32))
    blob_velocity = velocity.reshape(3, blob_count)
    plate_match = blob_platelet[:, None] == jnp.arange(plate_count, dtype=jnp.int32)[None, :]
    slot_of = jnp.sum(jnp.where(plate_match, platelet_owner[None, :], 0), axis=1)
    whole_body = PLAT_DEV * PB
    region_target = jnp.where(is_live, slot_of * PB + blob_rank, plate_count * PB)
    all_velocity, all_target = (
        lax.all_gather(blob_velocity, "member", axis=1, tiled=True),
        lax.all_gather(region_target, "member", axis=0, tiled=True),
    )
    local_index = all_target - lax.axis_index("member") * whole_body
    local_index = jnp.where(
        (local_index >= 0) & (local_index < whole_body), local_index, whole_body
    )
    body_flat = (
        jnp.zeros((3, whole_body), jnp.float32).at[:, local_index].set(all_velocity, mode="drop")
    )
    body_in = (
        body_flat.reshape(3, PLAT_DEV, PB)
        .transpose(1, 0, 2)
        .reshape(PLAT_DEV, 3 * PB)
        .astype(jnp.bfloat16)
    )
    body_velocity = jnp.einsum(
        "pab,pb->pa", preconditioner, body_in, preferred_element_type=jnp.float32
    )
    return (blob_velocity, body_velocity)


def solution(mesh):
    placed = (
        P(None, ("region", "member")),
        P(None, ("region", "member")),
        P(("region", "member")),
        P(("region", "member")),
        P("region"),
        P(("region", "member"), None),
        P(("region", "member")),
        P(("region", "member"), None, None),
    )
    return jax.shard_map(
        on_device,
        mesh=mesh,
        in_specs=placed,
        out_specs=(P(None, ("region", "member")), P(("region", "member"), None)),
        check_vma=False,
    )
```

profile of v0, /device:TPU:0, one launch (start us, length us, event | category | flops | bytes accessed | tf_op | source)
XLA Modules:
  0.0 66.3 jit_solution(10608921622263139967)
XLA Ops:
  0.7 0.9 %select_reduce_fusion = s32[384]{0:T(512)S(1)} fusion(s32[8]{0:T(128)} %param.17, s32[384]{0:T(512)} %param.15), kind=kLoop, calls=%fused_computation.62 | loop fusion | flops 8832 | bytes 3104 | tf_op jit(solution)/shard_map/reduce_sum | solution.py:91
  1.6 0.7 copy-done.6
  2.2 0.7 %copy-done.1 = f32[3,384]{1,0:T(4,128)S(1)} copy-done((f32[3,384]{1,0:T(4,128)S(1)}, f32[3,384]{1,0:T(4,128)}, u32[]{:S(2)}) %copy-start.1) | copy-done | bytes 4632
  2.9 9.7 %all_gather.9 = f32[6,1536]{1,0:T(8,128)S(1)} all-gather(f32[6,384]{1,0:T(8,128)S(1)} %pad_maximum_fusion), channel_id=1, replica_groups=mesh['region'=8,'member'=4] {'member'}, dimensions={1}, use_global_device_ids=true | all-gather | bytes 46080 | tf_op jit(solution)/shard_map/all_gather | solution.py:76
  12.7 1.3 %collective-permute-start.1 = (f32[6,768]{1,0:T(8,128)S(1)}, f32[6,768]{1,0:T(8,128)S(1)}, u32[]{:S(2)}, u32[]{:S(2)}) collective-permute-start(f32[6,768]{1,0:T(8,128)S(1)} %get-tuple-element.180), channel_id=1, source_target_pairs={{4,0},{8,4},{12,8},{16,12},{20,16},{24,20},{28,24},{5,1},{9,5},{13... | collective-permute-start | bytes 55304 | tf_op jit(solution)/shard_map/ppermute | solution.py:23
  14.0 3.0 %collective-permute-start = (f32[6,768]{1,0:T(8,128)S(1)}, f32[6,768]{1,0:T(8,128)S(1)}, u32[]{:S(2)}, u32[]{:S(2)}) collective-permute-start(f32[6,768]{1,0:T(8,128)S(1)} %get-tuple-element.179), channel_id=1, source_target_pairs={{0,4},{4,8},{8,12},{12,16},{16,20},{20,24},{24,28},{1,5},{5,9},{9,... | collective-permute-start | bytes 55304 | tf_op jit(solution)/shard_map/ppermute | solution.py:21
  17.0 8.1 %all-gather = s32[4,1,384]{2,1,0:T(1,128)S(1)} all-gather(s32[1,1,384]{2,1,0:T(1,128)S(1)} %reshape.93), channel_id=1, replica_groups=mesh['region'=8,'member'=4] {'member'}, dimensions={0}, use_global_device_ids=true | all-gather | bytes 7680 | tf_op jit(solution)/shard_map/all_gather | solution.py:96
  25.2 0.7 copy-done.8
  25.9 0.6 copy-done.9
  26.5 0.6 reduce_max.9
  27.2 0.6 copy-done.3
  27.8 22.2 %while.13 = (s32[]{:T(128)}, f32[3,3,128]{2,1,0:T(4,128)S(1)}, s32[]{:T(128)}, s32[3]{0:T(128)S(1)}, f32[3,384]{1,0:T(4,128)}, /*index=5*/s32[3,8]{0,1:T(8,128)S...) while((s32[]{:T(128)}, f32[3,3,128]{2,1,0:T(4,128)S(1)}, ...), condition=%wide.wide.region_8.9_spmd.clone.clone, body=%wide.wide.region_1.8_spmd.sunk.clone.clone.sunk | while | flops 6790173 | bytes 6481697 | solution.py:88
  28.5 0.6 gather_fusion
  29.2 0.3 fusion.34
  29.8 1.0 %fusion.35 = f32[3,3,128]{2,1,0:T(4,128)S(1)} fusion(f32[3,128,128]{2,1,0:T(8,128)S(1)} %get-tuple-element.308, f32[3,128,128]{2,1,0:T(8,128)S(1)} %get-tuple-element.311, f32[3,128,128]{2,1,0:T(8,128)S(1)} %get-tuple-element.312, f32[3,128]{1,0:T(4,128)S(1)} %get-tuple-element.313, f32[3,128,128]{2,1,0:T(8,128)S(1)} %slice_bitcast_fusion.3, ...), kind=kLoop, calls=%fused_computation.17.clone.clone.1 | loop fusion | flops 4717440 | bytes 2194956 | tf_op jit(solution)/shard_map/while/body/reduce_sum | solution.py:58
  31.6 0.6 gather_fusion
  32.3 0.3 fusion.34
  32.9 1.0 %fusion.35 = f32[3,3,128]{2,1,0:T(4,128)S(1)} fusion(f32[3,128,128]{2,1,0:T(8,128)S(1)} %get-tuple-element.308, f32[3,128,128]{2,1,0:T(8,128)S(1)} %get-tuple-element.311, f32[3,128,128]{2,1,0:T(8,128)S(1)} %get-tuple-element.312, f32[3,128]{1,0:T(4,128)S(1)} %get-tuple-element.313, f32[3,128,128]{2,1,0:T(8,128)S(1)} %slice_bitcast_fusion.3, ...), kind=kLoop, calls=%fused_computation.17.clone.clone.1 | loop fusion | flops 4717440 | bytes 2194956 | tf_op jit(solution)/shard_map/while/body/reduce_sum | solution.py:58
  34.7 0.6 gather_fusion
  35.9 1.0 %fusion.35 = f32[3,3,128]{2,1,0:T(4,128)S(1)} fusion(f32[3,128,128]{2,1,0:T(8,128)S(1)} %get-tuple-element.308, f32[3,128,128]{2,1,0:T(8,128)S(1)} %get-tuple-element.311, f32[3,128,128]{2,1,0:T(8,128)S(1)} %get-tuple-element.312, f32[3,128]{1,0:T(4,128)S(1)} %get-tuple-element.313, f32[3,128,128]{2,1,0:T(8,128)S(1)} %slice_bitcast_fusion.3, ...), kind=kLoop, calls=%fused_computation.17.clone.clone.1 | loop fusion | flops 4717440 | bytes 2194956 | tf_op jit(solution)/shard_map/while/body/reduce_sum | solution.py:58
  37.7 0.6 gather_fusion
  39.0 1.0 %fusion.35 = f32[3,3,128]{2,1,0:T(4,128)S(1)} fusion(f32[3,128,128]{2,1,0:T(8,128)S(1)} %get-tuple-element.308, f32[3,128,128]{2,1,0:T(8,128)S(1)} %get-tuple-element.311, f32[3,128,128]{2,1,0:T(8,128)S(1)} %get-tuple-element.312, f32[3,128]{1,0:T(4,128)S(1)} %get-tuple-element.313, f32[3,128,128]{2,1,0:T(8,128)S(1)} %slice_bitcast_fusion.3, ...), kind=kLoop, calls=%fused_computation.17.clone.clone.1 | loop fusion | flops 4717440 | bytes 2194956 | tf_op jit(solution)/shard_map/while/body/reduce_sum | solution.py:58
  40.8 0.6 gather_fusion
  42.1 1.0 %fusion.35 = f32[3,3,128]{2,1,0:T(4,128)S(1)} fusion(f32[3,128,128]{2,1,0:T(8,128)S(1)} %get-tuple-element.308, f32[3,128,128]{2,1,0:T(8,128)S(1)} %get-tuple-element.311, f32[3,128,128]{2,1,0:T(8,128)S(1)} %get-tuple-element.312, f32[3,128]{1,0:T(4,128)S(1)} %get-tuple-element.313, f32[3,128,128]{2,1,0:T(8,128)S(1)} %slice_bitcast_fusion.3, ...), kind=kLoop, calls=%fused_computation.17.clone.clone.1 | loop fusion | flops 4717440 | bytes 2194956 | tf_op jit(solution)/shard_map/while/body/reduce_sum | solution.py:58
  43.9 0.6 gather_fusion
  45.2 1.0 %fusion.35 = f32[3,3,128]{2,1,0:T(4,128)S(1)} fusion(f32[3,128,128]{2,1,0:T(8,128)S(1)} %get-tuple-element.308, f32[3,128,128]{2,1,0:T(8,128)S(1)} %get-tuple-element.311, f32[3,128,128]{2,1,0:T(8,128)S(1)} %get-tuple-element.312, f32[3,128]{1,0:T(4,128)S(1)} %get-tuple-element.313, f32[3,128,128]{2,1,0:T(8,128)S(1)} %slice_bitcast_fusion.3, ...), kind=kLoop, calls=%fused_computation.17.clone.clone.1 | loop fusion | flops 4717440 | bytes 2194956 | tf_op jit(solution)/shard_map/while/body/reduce_sum | solution.py:58
  47.0 0.6 gather_fusion
  48.3 1.0 %fusion.35 = f32[3,3,128]{2,1,0:T(4,128)S(1)} fusion(f32[3,128,128]{2,1,0:T(8,128)S(1)} %get-tuple-element.308, f32[3,128,128]{2,1,0:T(8,128)S(1)} %get-tuple-element.311, f32[3,128,128]{2,1,0:T(8,128)S(1)} %get-tuple-element.312, f32[3,128]{1,0:T(4,128)S(1)} %get-tuple-element.313, f32[3,128,128]{2,1,0:T(8,128)S(1)} %slice_bitcast_fusion.3, ...), kind=kLoop, calls=%fused_computation.17.clone.clone.1 | loop fusion | flops 4717440 | bytes 2194956 | tf_op jit(solution)/shard_map/while/body/reduce_sum | solution.py:58
  50.1 10.3 %all_gather.11 = f32[3,1536]{1,0:T(4,128)S(1)} all-gather(f32[3,384]{1,0:T(4,128)S(1)} %bitcast.48), channel_id=1, replica_groups=mesh['region'=8,'member'=4] {'member'}, dimensions={1}, use_global_device_ids=true | all-gather | bytes 23040 | tf_op jit(solution)/shard_map/all_gather | solution.py:95
  60.7 4.4 %scatter_custom_fusion = f32[3,324]{0,1:T(8,128)S(1)} fusion(s32[1536]{0:T(1024)S(1)} %compare_select_fusion.1, f32[1536,3]{1,0:T(8,128)S(1)} %copy.44, f32[]{:T(128)} %constant.14.clone.1), kind=kCustom, calls=%fused_computation.58 | custom fusion | bytes 3892 | tf_op jit(solution)/shard_map/scatter | solution.py:103
  65.3 0.4 fusion.24
  65.7 0.6 copy.63
  (161 shorter events, 5.4 us)
Async XLA Ops:
  0.6 64.7 %copy-start = (bf16[2,486,486]{2,0,1:T(2,128)(2,1)S(1)}, bf16[2,486,486]{2,0,1:T(2,128)(2,1)}, u32[]{:S(2)}) copy-start(bf16[2,486,486]{2,0,1:T(2,128)(2,1)} %param.20) | copy-start | bytes 2834356
  0.6 0.9 %copy-start.5 = (s32[384]{0:T(512)S(1)}, s32[384]{0:T(512)}, u32[]{:S(2)}) copy-start(s32[384]{0:T(512)} %param.15) | copy-start | bytes 4612
  0.7 0.9 %copy-start.7 = (s32[384]{0:T(512)S(1)}, s32[384]{0:T(512)}, u32[]{:S(2)}) copy-start(s32[384]{0:T(512)} %param.16) | copy-start | bytes 4612
  1.5 0.7 %copy-start.6 = (f32[3,384]{1,0:T(4,128)S(1)}, f32[3,384]{1,0:T(4,128)}, u32[]{:S(2)}) copy-start(f32[3,384]{1,0:T(4,128)} %param.14) | copy-start | bytes 13828
  2.2 0.7 %copy-start.1 = (f32[3,384]{1,0:T(4,128)S(1)}, f32[3,384]{1,0:T(4,128)}, u32[]{:S(2)}) copy-start(f32[3,384]{1,0:T(4,128)} %param.13) | copy-start | bytes 13828
  12.7 14.5 %collective-permute-start.1 = (f32[6,768]{1,0:T(8,128)S(1)}, f32[6,768]{1,0:T(8,128)S(1)}, u32[]{:S(2)}, u32[]{:S(2)}) collective-permute-start(f32[6,768]{1,0:T(8,128)S(1)} %get-tuple-element.180), channel_id=1, source_target_pairs={{4,0},{8,4},{12,8},{16,12},{20,16},{24,20},{28,24},{5,1},{9,5},{13... | collective-permute-start | bytes 55304 | tf_op jit(solution)/shard_map/ppermute | solution.py:23
  14.0 13.2 %collective-permute-start = (f32[6,768]{1,0:T(8,128)S(1)}, f32[6,768]{1,0:T(8,128)S(1)}, u32[]{:S(2)}, u32[]{:S(2)}) collective-permute-start(f32[6,768]{1,0:T(8,128)S(1)} %get-tuple-element.179), channel_id=1, source_target_pairs={{0,4},{4,8},{8,12},{12,16},{16,20},{20,24},{24,28},{1,5},{5,9},{9,... | collective-permute-start | bytes 55304 | tf_op jit(solution)/shard_map/ppermute | solution.py:21
  25.1 0.7 %copy-start.8 = (s32[3,8]{1,0:T(4,128)S(1)}, s32[3,8]{1,0:T(4,128)}, u32[]{:S(2)}) copy-start(s32[3,8]{1,0:T(4,128)} %param.18) | copy-start | bytes 292
  25.8 0.7 copy-start.9
  27.1 0.7 copy-start.3
  27.1 0.7 copy-start.4
  50.0 10.3 %copy-start.2 = (f32[1,3,3,128]{3,1,2,0:T(4,128)}, f32[1,3,3,128]{3,1,2,0:T(4,128)S(1)}, u32[]{:S(2)}) copy-start(f32[1,3,3,128]{3,1,2,0:T(4,128)S(1)} %copy.62) | copy-start | bytes 13828
where the time goes:
time: 66.8 us; the launch traced here: 66.3 us
  blocking collectives  28.1 us (42%)
  other arithmetic  13.6 us (20%)
  local copies, waits for them, and re-layouts  13 us (19%)
  loops' own time  6.05 us (9%)
  starting transfers between devices  4.32 us (6%)
  between operations  0.83 us (1%)
    all_gather x1, blocking collectives, on_device(): lax.all_gather(blob_velocity, 'member', axis=1, tiled=True)  10.3 us
    all_gather x1, blocking collectives, on_device(): region_all = lax.all_gather(own_blobs, 'member', axis=1, tiled=True)  9.71 us
    all_gather x1, blocking collectives, on_device(): lax.all_gather(region_target, 'member', axis=0, tiled=True)  8.06 us
    reduce_sum x7, other arithmetic, stokes_sum(): return jnp.sum(direct + wall_term, axis=3)  7.13 us
    another operation x1, loops' own time, on_device(): lax.fori_loop(0, pair_rounds, one_slot, jnp.zeros(targets.shape, jnp.floa...  6.05 us
    scatter x1, local copies, waits for them, and re-layouts, on_device(): jnp.zeros((3, whole_body), jnp.float32).at[:, local_index]  4.36 us
    gather x7, local copies, waits for them, and re-layouts, one_slot(): picked = jnp.take(ext_blocks, source_ids, axis=1)  3.85 us
    unnamed x24, local copies, waits for them, and re-layouts  3.43 us
  transfers between devices with their start and end apart: 2, of which 0 were waited for; matrix products, arithmetic and copies ran while one was open for 1% of the time, Pallas kernels for 0%

commit v1 on v0

--- a/solution.py
+++ b/solution.py
@@ -73,7 +73,14 @@
     is_live = blob_platelet < plate_count
     live_mask = is_live.astype(jnp.float32)
     own_blobs = jnp.concatenate([positions, forces * live_mask[None, :]], 0)
-    region_all = lax.all_gather(own_blobs, "member", axis=1, tiled=True)
+    ring = [own_blobs]
+    for hop in range(3):
+        ring.append(lax.ppermute(ring[-1], "member", [(dev, (dev + 1) % 4) for dev in range(4)]))
+    region_all = jnp.roll(
+        jnp.concatenate(ring[::-1], axis=1),
+        (lax.axis_index("member") + 1) * ring[0].shape[1],
+        axis=1,
+    )
     extended = padded(region_all, (("region", 1),), region_all.shape[1] // 2)
     ext_blocks = extended.reshape(6, extended.shape[1] // TILE, TILE)
     targets = positions.reshape(3, blob_count // TILE, TILE)

time: 66.8 us -> 68.8 us (1.030)
  the two profiles are of different devices: /device:TPU:0 before, /device:TPU:26 now
where the time goes in v1:
time: 68.8 us; the launch traced here: 68.3 us
  blocking collectives  16.4 us (24%)
  other arithmetic  15.4 us (22%)
  local copies, waits for them, and re-layouts  13.9 us (20%)
  starting transfers between devices  9.83 us (14%)
  loops' own time  6.82 us (10%)
  waiting for transfers between devices  4.84 us (7%)
  between operations  0.85 us (1%)
    all_gather x1, blocking collectives, on_device(): lax.all_gather(blob_velocity, 'member', axis=1, tiled=True)  9.27 us
    reduce_sum x8, other arithmetic, stokes_sum(): return jnp.sum(direct + wall_term, axis=3)  8.14 us
    all_gather x1, blocking collectives, on_device(): lax.all_gather(region_target, 'member', axis=0, tiled=True)  7.09 us
    another operation x1, loops' own time, on_device(): lax.fori_loop(0, pair_rounds, one_slot, jnp.zeros(targets.shape, jnp.floa...  6.82 us
    ppermute x3, starting transfers between devices, on_device(): lax.ppermute(ring[-1], 'member', [(dev, (dev + 1) % 4) for dev in range(4)])  5.51 us
    gather x8, local copies, waits for them, and re-layouts, one_slot(): picked = jnp.take(ext_blocks, source_ids, axis=1)  4.4 us
    scatter x1, local copies, waits for them, and re-layouts, on_device(): jnp.zeros((3, whole_body), jnp.float32).at[:, local_index]  4.36 us
    unnamed x30, local copies, waits for them, and re-layouts  3.53 us
  transfers between devices with their start and end apart: 5, of which 2 were waited for; matrix products, arithmetic and copies ran while one was open for 1% of the time, Pallas kernels for 0%

profile of v1, /device:TPU:26, one launch (start us, length us, event | category | flops | bytes accessed | tf_op | source)
XLA Modules:
  0.0 68.3 jit_solution(18182112019168442217)
XLA Ops:
  0.7 0.9 %select_reduce_fusion = s32[384]{0:T(512)S(1)} fusion(s32[8]{0:T(128)} %param.17, s32[384]{0:T(512)} %param.15), kind=kLoop, calls=%fused_computation.70 | loop fusion | flops 8832 | bytes 3104 | tf_op jit(solution)/shard_map/reduce_sum | solution.py:98
  1.6 0.7 copy-done.6
  2.2 0.7 %copy-done.1 = f32[3,384]{1,0:T(4,128)S(1)} copy-done((f32[3,384]{1,0:T(4,128)S(1)}, f32[3,384]{1,0:T(4,128)}, u32[]{:S(2)}) %copy-start.1) | copy-done | bytes 4632
  2.9 1.5 %collective-permute-start = (f32[6,384]{1,0:T(8,128)S(1)}, f32[6,384]{1,0:T(8,128)S(1)}, u32[]{:S(2)}, u32[]{:S(2)}) collective-permute-start(f32[6,384]{1,0:T(8,128)S(1)} %pad_maximum_fusion), channel_id=1, source_target_pairs={{0,1},{1,2},{2,3},{3,0},{4,5},{5,6},{6,7},{7,4},{8,9},{9,10},{10,1... | collective-permute-start | bytes 27656 | tf_op jit(solution)/shard_map/ppermute | solution.py:78
  4.5 7.1 %all-gather = s32[4,1,384]{2,1,0:T(1,128)S(1)} all-gather(s32[1,1,384]{2,1,0:T(1,128)S(1)} %reshape.93), channel_id=1, replica_groups=mesh['region'=8,'member'=4] {'member'}, dimensions={0}, use_global_device_ids=true | all-gather | bytes 7680 | tf_op jit(solution)/shard_map/all_gather | solution.py:103
  11.6 1.5 %collective-permute-start.1 = (f32[6,384]{1,0:T(8,128)S(1)}, f32[6,384]{1,0:T(8,128)S(1)}, u32[]{:S(2)}, u32[]{:S(2)}) collective-permute-start(f32[6,384]{1,0:T(8,128)S(1)} %collective-permute-done), channel_id=1, source_target_pairs={{0,1},{1,2},{2,3},{3,0},{4,5},{5,6},{6,7},{7,4},{8,9},{9,10},{10,1... | collective-permute-start | bytes 27656 | tf_op jit(solution)/shard_map/ppermute | solution.py:78
  13.1 2.2 %collective-permute-done.1 = f32[6,384]{1,0:T(8,128)S(1)} collective-permute-done((f32[6,384]{1,0:T(8,128)S(1)}, f32[6,384]{1,0:T(8,128)S(1)}, u32[]{:S(2)}, u32[]{:S(2)}) %collective-permute-start.1) | collective-permute-done | bytes 9248 | tf_op jit(solution)/shard_map/ppermute | solution.py:78
  15.3 2.5 %collective-permute-start.2 = (f32[6,384]{1,0:T(8,128)S(1)}, f32[6,384]{1,0:T(8,128)S(1)}, u32[]{:S(2)}, u32[]{:S(2)}) collective-permute-start(f32[6,384]{1,0:T(8,128)S(1)} %collective-permute-done.1), channel_id=1, source_target_pairs={{0,1},{1,2},{2,3},{3,0},{4,5},{5,6},{6,7},{7,4},{8,9},{9,10},{10,1... | collective-permute-start | bytes 27656 | tf_op jit(solution)/shard_map/ppermute | solution.py:78
  17.8 0.7 copy-done.8
  18.5 0.7 copy-done.9
  19.2 0.6 reduce_max.9
  20.0 1.9 %collective-permute-start.4 = (f32[6,768]{1,0:T(8,128)S(1)}, f32[6,768]{1,0:T(8,128)S(1)}, u32[]{:S(2)}, u32[]{:S(2)}) collective-permute-start(f32[6,768]{1,0:T(8,128)S(1)} %get-tuple-element.180), channel_id=1, source_target_pairs={{4,0},{8,4},{12,8},{16,12},{20,16},{24,20},{28,24},{5,1},{9,5},{13... | collective-permute-start | bytes 55304 | tf_op jit(solution)/shard_map/ppermute | solution.py:23
  21.9 2.4 %collective-permute-start.3 = (f32[6,768]{1,0:T(8,128)S(1)}, f32[6,768]{1,0:T(8,128)S(1)}, u32[]{:S(2)}, u32[]{:S(2)}) collective-permute-start(f32[6,768]{1,0:T(8,128)S(1)} %get-tuple-element.179), channel_id=1, source_target_pairs={{0,4},{4,8},{8,12},{12,16},{16,20},{20,24},{24,28},{1,5},{5,9},{9,... | collective-permute-start | bytes 55304 | tf_op jit(solution)/shard_map/ppermute | solution.py:21
  24.4 2.6 %collective-permute-done.3 = f32[6,768]{1,0:T(8,128)S(1)} collective-permute-done((f32[6,768]{1,0:T(8,128)S(1)}, f32[6,768]{1,0:T(8,128)S(1)}, u32[]{:S(2)}, u32[]{:S(2)}) %collective-permute-start.3) | collective-permute-done | bytes 18464 | tf_op jit(solution)/shard_map/ppermute | solution.py:21
  27.1 0.6 copy-done.3
  27.8 25.3 %while.13 = (s32[]{:T(128)}, f32[3,3,128]{2,1,0:T(4,128)S(1)}, s32[]{:T(128)}, s32[3]{0:T(128)S(1)}, f32[3,384]{1,0:T(4,128)}, /*index=5*/s32[3,8]{0,1:T(8,128)S...) while((s32[]{:T(128)}, f32[3,3,128]{2,1,0:T(4,128)S(1)}, ...), condition=%wide.wide.region_8.9_spmd.clone.clone, body=%wide.wide.region_1.8_spmd.sunk.clone.clone.sunk | while | flops 6790173 | bytes 6481697 | solution.py:95
  28.5 0.6 gather_fusion
  29.7 1.0 %fusion.34 = f32[3,3,128]{2,1,0:T(4,128)S(1)} fusion(f32[3,128,128]{2,1,0:T(8,128)S(1)} %get-tuple-element.308, f32[3,128,128]{2,1,0:T(8,128)S(1)} %get-tuple-element.311, f32[3,128,128]{2,1,0:T(8,128)S(1)} %get-tuple-element.312, f32[3,128]{1,0:T(4,128)S(1)} %get-tuple-element.313, f32[3,128,128]{2,1,0:T(8,128)S(1)} %slice_bitcast_fusion.3, ...), kind=kLoop, calls=%fused_computation.17.clone.clone.1 | loop fusion | flops 4717440 | bytes 2194956 | tf_op jit(solution)/shard_map/while/body/reduce_sum | solution.py:58
  31.5 0.6 gather_fusion
  32.8 1.0 %fusion.34 = f32[3,3,128]{2,1,0:T(4,128)S(1)} fusion(f32[3,128,128]{2,1,0:T(8,128)S(1)} %get-tuple-element.308, f32[3,128,128]{2,1,0:T(8,128)S(1)} %get-tuple-element.311, f32[3,128,128]{2,1,0:T(8,128)S(1)} %get-tuple-element.312, f32[3,128]{1,0:T(4,128)S(1)} %get-tuple-element.313, f32[3,128,128]{2,1,0:T(8,128)S(1)} %slice_bitcast_fusion.3, ...), kind=kLoop, calls=%fused_computation.17.clone.clone.1 | loop fusion | flops 4717440 | bytes 2194956 | tf_op jit(solution)/shard_map/while/body/reduce_sum | solution.py:58
  34.6 0.6 gather_fusion
  35.9 1.0 %fusion.34 = f32[3,3,128]{2,1,0:T(4,128)S(1)} fusion(f32[3,128,128]{2,1,0:T(8,128)S(1)} %get-tuple-element.308, f32[3,128,128]{2,1,0:T(8,128)S(1)} %get-tuple-element.311, f32[3,128,128]{2,1,0:T(8,128)S(1)} %get-tuple-element.312, f32[3,128]{1,0:T(4,128)S(1)} %get-tuple-element.313, f32[3,128,128]{2,1,0:T(8,128)S(1)} %slice_bitcast_fusion.3, ...), kind=kLoop, calls=%fused_computation.17.clone.clone.1 | loop fusion | flops 4717440 | bytes 2194956 | tf_op jit(solution)/shard_map/while/body/reduce_sum | solution.py:58
  37.7 0.6 gather_fusion
  39.0 1.0 %fusion.34 = f32[3,3,128]{2,1,0:T(4,128)S(1)} fusion(f32[3,128,128]{2,1,0:T(8,128)S(1)} %get-tuple-element.308, f32[3,128,128]{2,1,0:T(8,128)S(1)} %get-tuple-element.311, f32[3,128,128]{2,1,0:T(8,128)S(1)} %get-tuple-element.312, f32[3,128]{1,0:T(4,128)S(1)} %get-tuple-element.313, f32[3,128,128]{2,1,0:T(8,128)S(1)} %slice_bitcast_fusion.3, ...), kind=kLoop, calls=%fused_computation.17.clone.clone.1 | loop fusion | flops 4717440 | bytes 2194956 | tf_op jit(solution)/shard_map/while/body/reduce_sum | solution.py:58
  40.8 0.6 gather_fusion
  42.1 1.0 %fusion.34 = f32[3,3,128]{2,1,0:T(4,128)S(1)} fusion(f32[3,128,128]{2,1,0:T(8,128)S(1)} %get-tuple-element.308, f32[3,128,128]{2,1,0:T(8,128)S(1)} %get-tuple-element.311, f32[3,128,128]{2,1,0:T(8,128)S(1)} %get-tuple-element.312, f32[3,128]{1,0:T(4,128)S(1)} %get-tuple-element.313, f32[3,128,128]{2,1,0:T(8,128)S(1)} %slice_bitcast_fusion.3, ...), kind=kLoop, calls=%fused_computation.17.clone.clone.1 | loop fusion | flops 4717440 | bytes 2194956 | tf_op jit(solution)/shard_map/while/body/reduce_sum | solution.py:58
  45.1 1.0 %fusion.34 = f32[3,3,128]{2,1,0:T(4,128)S(1)} fusion(f32[3,128,128]{2,1,0:T(8,128)S(1)} %get-tuple-element.308, f32[3,128,128]{2,1,0:T(8,128)S(1)} %get-tuple-element.311, f32[3,128,128]{2,1,0:T(8,128)S(1)} %get-tuple-element.312, f32[3,128]{1,0:T(4,128)S(1)} %get-tuple-element.313, f32[3,128,128]{2,1,0:T(8,128)S(1)} %slice_bitcast_fusion.3, ...), kind=kLoop, calls=%fused_computation.17.clone.clone.1 | loop fusion | flops 4717440 | bytes 2194956 | tf_op jit(solution)/shard_map/while/body/reduce_sum | solution.py:58
  48.2 1.0 %fusion.34 = f32[3,3,128]{2,1,0:T(4,128)S(1)} fusion(f32[3,128,128]{2,1,0:T(8,128)S(1)} %get-tuple-element.308, f32[3,128,128]{2,1,0:T(8,128)S(1)} %get-tuple-element.311, f32[3,128,128]{2,1,0:T(8,128)S(1)} %get-tuple-element.312, f32[3,128]{1,0:T(4,128)S(1)} %get-tuple-element.313, f32[3,128,128]{2,1,0:T(8,128)S(1)} %slice_bitcast_fusion.3, ...), kind=kLoop, calls=%fused_computation.17.clone.clone.1 | loop fusion | flops 4717440 | bytes 2194956 | tf_op jit(solution)/shard_map/while/body/reduce_sum | solution.py:58
  51.3 1.0 %fusion.34 = f32[3,3,128]{2,1,0:T(4,128)S(1)} fusion(f32[3,128,128]{2,1,0:T(8,128)S(1)} %get-tuple-element.308, f32[3,128,128]{2,1,0:T(8,128)S(1)} %get-tuple-element.311, f32[3,128,128]{2,1,0:T(8,128)S(1)} %get-tuple-element.312, f32[3,128]{1,0:T(4,128)S(1)} %get-tuple-element.313, f32[3,128,128]{2,1,0:T(8,128)S(1)} %slice_bitcast_fusion.3, ...), kind=kLoop, calls=%fused_computation.17.clone.clone.1 | loop fusion | flops 4717440 | bytes 2194956 | tf_op jit(solution)/shard_map/while/body/reduce_sum | solution.py:58
  53.1 9.3 %all_gather.7 = f32[3,1536]{1,0:T(4,128)S(1)} all-gather(f32[3,384]{1,0:T(4,128)S(1)} %bitcast.48), channel_id=1, replica_groups=mesh['region'=8,'member'=4] {'member'}, dimensions={1}, use_global_device_ids=true | all-gather | bytes 23040 | tf_op jit(solution)/shard_map/all_gather | solution.py:102
  62.7 4.4 %scatter_custom_fusion = f32[3,324]{0,1:T(8,128)S(1)} fusion(s32[1536]{0:T(1024)S(1)} %compare_select_fusion.1, f32[1536,3]{1,0:T(8,128)S(1)} %copy.44, f32[]{:T(128)} %constant.42.clone.1), kind=kCustom, calls=%fused_computation.58 | custom fusion | bytes 3892 | tf_op jit(solution)/shard_map/scatter | solution.py:110
  67.7 0.6 copy.63
  (195 shorter events, 9.0 us)
Async XLA Ops:
  0.6 66.7 %copy-start = (bf16[2,486,486]{2,0,1:T(2,128)(2,1)S(1)}, bf16[2,486,486]{2,0,1:T(2,128)(2,1)}, u32[]{:S(2)}) copy-start(bf16[2,486,486]{2,0,1:T(2,128)(2,1)} %param.20) | copy-start | bytes 2834356
  0.6 0.9 %copy-start.5 = (s32[384]{0:T(512)S(1)}, s32[384]{0:T(512)}, u32[]{:S(2)}) copy-start(s32[384]{0:T(512)} %param.15) | copy-start | bytes 4612
  0.7 0.9 %copy-start.7 = (s32[384]{0:T(512)S(1)}, s32[384]{0:T(512)}, u32[]{:S(2)}) copy-start(s32[384]{0:T(512)} %param.16) | copy-start | bytes 4612
  1.5 0.7 %copy-start.6 = (f32[3,384]{1,0:T(4,128)S(1)}, f32[3,384]{1,0:T(4,128)}, u32[]{:S(2)}) copy-start(f32[3,384]{1,0:T(4,128)} %param.14) | copy-start | bytes 13828
  2.2 0.7 %copy-start.1 = (f32[3,384]{1,0:T(4,128)S(1)}, f32[3,384]{1,0:T(4,128)}, u32[]{:S(2)}) copy-start(f32[3,384]{1,0:T(4,128)} %param.13) | copy-start | bytes 13828
  2.9 8.6 %collective-permute-start = (f32[6,384]{1,0:T(8,128)S(1)}, f32[6,384]{1,0:T(8,128)S(1)}, u32[]{:S(2)}, u32[]{:S(2)}) collective-permute-start(f32[6,384]{1,0:T(8,128)S(1)} %pad_maximum_fusion), channel_id=1, source_target_pairs={{0,1},{1,2},{2,3},{3,0},{4,5},{5,6},{6,7},{7,4},{8,9},{9,10},{10,1... | collective-permute-start | bytes 27656 | tf_op jit(solution)/shard_map/ppermute | solution.py:78
  11.6 3.7 %collective-permute-start.1 = (f32[6,384]{1,0:T(8,128)S(1)}, f32[6,384]{1,0:T(8,128)S(1)}, u32[]{:S(2)}, u32[]{:S(2)}) collective-permute-start(f32[6,384]{1,0:T(8,128)S(1)} %collective-permute-done), channel_id=1, source_target_pairs={{0,1},{1,2},{2,3},{3,0},{4,5},{5,6},{6,7},{7,4},{8,9},{9,10},{10,1... | collective-permute-start | bytes 27656 | tf_op jit(solution)/shard_map/ppermute | solution.py:78
  15.3 4.5 %collective-permute-start.2 = (f32[6,384]{1,0:T(8,128)S(1)}, f32[6,384]{1,0:T(8,128)S(1)}, u32[]{:S(2)}, u32[]{:S(2)}) collective-permute-start(f32[6,384]{1,0:T(8,128)S(1)} %collective-permute-done.1), channel_id=1, source_target_pairs={{0,1},{1,2},{2,3},{3,0},{4,5},{5,6},{6,7},{7,4},{8,9},{9,10},{10,1... | collective-permute-start | bytes 27656 | tf_op jit(solution)/shard_map/ppermute | solution.py:78
  17.8 0.7 copy-start.8
  18.5 0.7 copy-start.9
  20.0 4.4 %collective-permute-start.4 = (f32[6,768]{1,0:T(8,128)S(1)}, f32[6,768]{1,0:T(8,128)S(1)}, u32[]{:S(2)}, u32[]{:S(2)}) collective-permute-start(f32[6,768]{1,0:T(8,128)S(1)} %get-tuple-element.180), channel_id=1, source_target_pairs={{4,0},{8,4},{12,8},{16,12},{20,16},{24,20},{28,24},{5,1},{9,5},{13... | collective-permute-start | bytes 55304 | tf_op jit(solution)/shard_map/ppermute | solution.py:23
  21.9 5.1 %collective-permute-start.3 = (f32[6,768]{1,0:T(8,128)S(1)}, f32[6,768]{1,0:T(8,128)S(1)}, u32[]{:S(2)}, u32[]{:S(2)}) collective-permute-start(f32[6,768]{1,0:T(8,128)S(1)} %get-tuple-element.179), channel_id=1, source_target_pairs={{0,4},{4,8},{8,12},{12,16},{16,20},{20,24},{24,28},{1,5},{5,9},{9,... | collective-permute-start | bytes 55304 | tf_op jit(solution)/shard_map/ppermute | solution.py:21
  27.1 0.7 copy-start.3
  27.1 0.7 copy-start.4
  53.1 9.3 %copy-start.2 = (f32[1,3,3,128]{3,1,2,0:T(4,128)}, f32[1,3,3,128]{3,1,2,0:T(4,128)S(1)}, u32[]{:S(2)}) copy-start(f32[1,3,3,128]{3,1,2,0:T(4,128)S(1)} %copy.62) | copy-start | bytes 13828
